TPU v7x, 512 devices: a whole 4x8x8 slice. The times are simulated.
512 devices in a mesh: expert: 8 (over x, core), tensor: 64 (over y, z).
Axes of the slice: x: 4, y: 8, z: 8, core: 2. Of those that a mesh axis runs over, the one named last changes fastest.
Arguments:
- tokens: bfloat16 [1536, 6144], P('tensor'), may hold values from -6 to 6
- expert_ids: int32 [1536, 2], P('tensor'), may hold values from 0 to 7, all different within a row; in each aligned block of 24 rows (0 to 23, 24 to 47, ...) at most 12 rows name the same one
- gate_units: int32 [1536, 2], P('tensor'), may hold values from 1 to 65535
- gate_weight: bfloat16 [8, 6144, 8192], P('expert', None, 'tensor'), may hold values from -0.078125 to 0.078125
- up_weight: bfloat16 [8, 6144, 8192], P('expert', None, 'tensor'), may hold values from -0.078125 to 0.078125
- down_weight: bfloat16 [8, 6144, 8192], P('expert', 'tensor'), may hold values from -0.0625 to 0.0625
Outputs:
- expert_mix: bfloat16 [1536, 6144], P('tensor', 'expert')
Inputs may be any that keep to these rules, and one draw needn't show every extreme that they name: `expert_ids`: within each aligned block of 24 rows (the tokens of one tensor index) the two ids of a row differ and no expert is named by more than 12 rows; in every draw some expert is named by exactly 12 rows of some block, and every expert is named somewhere.
All inputs are finite; a program needn't handle non-finite values.
Results may differ from a plain program's by a relative error of at most 0.0057.
Values may be sent and summed in bfloat16 or wider, within the bound.
A program may use at most 128 MiB of HBM per device.

v0:
```python
import jax
import jax.numpy as jnp
from jax import lax
from jax.sharding import PartitionSpec as P


def slot_tables(expert_ids, gate_units, expert_id, capacity):
    tok_rows = expert_ids.shape[0]
    top_count = expert_ids.shape[1]
    flat_route = expert_ids.reshape(-1)
    matches = (flat_route == expert_id).astype(jnp.int32)
    slot_rank = jnp.cumsum(matches) - matches
    slot_ids = jnp.arange(capacity, dtype=jnp.int32)
    assignment = jnp.where(
        (slot_rank[None, :] == slot_ids[:, None]) & (matches[None, :] == 1), 1.0, 0.0
    ).astype(jnp.float32)
    positions = jnp.arange(tok_rows * top_count, dtype=jnp.int32) // top_count
    owners = (positions[:, None] == jnp.arange(tok_rows, dtype=jnp.int32)[None, :]).astype(
        jnp.float32
    )
    unit_vals = gate_units.astype(jnp.float32)
    shares = unit_vals / jnp.sum(unit_vals, axis=1, keepdims=True)
    picker = jnp.dot(
        assignment, owners, precision=lax.Precision.HIGHEST, preferred_element_type=jnp.float32
    )
    weighted = jnp.dot(
        assignment,
        owners * shares.reshape(-1)[:, None],
        precision=lax.Precision.HIGHEST,
        preferred_element_type=jnp.float32,
    )
    return (picker, weighted)


def local(tokens, expert_ids, gate_units, gate_weight, up_weight, down_weight):
    experts = lax.axis_size("expert")
    expert_id = lax.axis_index("expert")
    tok_rows = tokens.shape[0]
    capacity = min(tok_rows, 4 * tok_rows // experts)
    picker, weighted = slot_tables(expert_ids, gate_units, expert_id, capacity)
    picked = jnp.dot(
        picker.astype(jnp.bfloat16), tokens, preferred_element_type=jnp.float32
    ).astype(jnp.bfloat16)
    w_gate = gate_weight[0]
    w_up = up_weight[0]
    w_down = down_weight[0]
    shard_piece = lax.all_gather(picked, "tensor", axis=0, tiled=True)
    gate_vals = jnp.dot(shard_piece, w_gate, preferred_element_type=jnp.float32)
    up_vals = jnp.dot(shard_piece, w_up, preferred_element_type=jnp.float32)
    hidden = (jax.nn.silu(gate_vals) * up_vals).astype(jnp.bfloat16)
    gathered = lax.all_gather(hidden, "tensor", axis=1, tiled=True)
    projected = lax.dot_general(
        gathered, w_down, (((1,), (1,)), ((), ())), preferred_element_type=jnp.float32
    )
    outputs = projected.astype(jnp.bfloat16)
    returned = lax.all_to_all(outputs, "tensor", split_axis=0, concat_axis=1, tiled=True)
    contribution = lax.dot_general(
        weighted,
        returned.astype(jnp.float32),
        (((0,), (0,)), ((), ())),
        precision=lax.Precision.HIGHEST,
        preferred_element_type=jnp.float32,
    )
    summed_all = lax.psum(contribution, "expert")
    col_width = contribution.shape[1] // experts
    mixed = lax.dynamic_slice_in_dim(summed_all, expert_id * col_width, col_width, 1)
    return mixed.astype(jnp.bfloat16)


def solution(mesh):
    return jax.shard_map(
        local,
        mesh=mesh,
        in_specs=(
            P("tensor", None),
            P("tensor", None),
            P("tensor", None),
            P("expert", None, "tensor"),
            P("expert", None, "tensor"),
            P("expert", "tensor", None),
        ),
        out_specs=P("tensor", "expert"),
        check_vma=False,
    )
```

profile of v0, /device:TPU:56, one launch (start us, length us, event | category | flops | bytes accessed | tf_op | source)
XLA Modules:
  0.0 347.9 jit_solution(7697855502720402069)
XLA Ops:
  6.5 0.8 compare_convert_fusion
  7.3 0.1 copy.17
  7.4 0.1 reshape.76
  7.7 0.1 reduce
  7.8 0.2 convolution_convert_fusion.1
  8.0 1.8 fusion
  9.9 123.9 %all-gather.6.cloned.1.call-done = bf16[64,12,6144]{2,1,0:T(8,128)(2,1)} async-done(((bf16[1,12,6144]{2,1,0:T(8,128)(2,1)}), bf16[64,12,6144]{2,1,0:T(8,128)(2,1)}) %all-gather.6.cloned.1.call-update) | async-done | bytes 9437200 | tf_op jit(solution)/shard_map/all_gather | solution.py:47
  133.8 13.7 %reshape.78 = bf16[768,6144]{1,0:T(8,128)(2,1)} reshape(bf16[64,12,6144]{2,1,0:T(8,128)(2,1)} %all-gather.6.cloned.1.call-done) | data formatting | bytes 18874368
  147.6 6.1 %fusion.5 = f32[768,128]{1,0:T(8,128)S(1)} fusion(bf16[768,6144]{1,0:T(8,128)(2,1)} %reshape.78, bf16[1,6144,128]{2,1,0:T(8,128)(2,1)S(1)} %copy-done), kind=kOutput, calls=%fused_computation.6 | convolution fusion | flops 1207959552 | bytes 11403264 | tf_op jit(solution)/shard_map/dot_general | solution.py:48
  153.7 0.3 copy-done.1
  154.0 0.4 copy-done.4
  154.4 3.3 fusion.10
  157.7 123.6 %all-gather.4.cloned.1.call-done = bf16[768,8192]{1,0:T(8,128)(2,1)} async-done(((bf16[768,128]{1,0:T(8,128)(2,1)}), bf16[768,8192]{1,0:T(8,128)(2,1)}) %all-gather.4.cloned.1.call-update) | async-done | bytes 12582928 | tf_op jit(solution)/shard_map/all_gather | solution.py:51
  281.3 8.6 %fusion.13 = bf16[768,96]{0,1:T(8,128)(2,1)S(1)} fusion(bf16[768,8192]{1,0:T(8,128)(2,1)} %all-gather.4.cloned.1.call-done, bf16[1,96,8192]{2,1,0:T(8,128)(2,1)S(1)} %copy-done.2), kind=kOutput, calls=%fused_computation.10 | convolution fusion | flops 1208033280 | bytes 14303232 | tf_op jit(solution)/shard_map/dot_general | solution.py:52
  289.9 0.2 copy.21
  290.1 0.8 all_to_all.14
  290.8 8.6 %all-to-all-start = ((bf16[64,12,96]{2,1,0:T(8,128)(2,1)}), bf16[64,12,96]{2,1,0:T(8,128)(2,1)S(1)}, u32[]{:S(2)}, u32[]{:S(2)}) async-start(bf16[64,12,96]{2,1,0:T(8,128)(2,1)} %all_to_all.14), calls=%async_computation | async-start | bytes 524288 | tf_op jit(solution)/shard_map/all_to_all | solution.py:56
  299.5 0.1 mul.20
  299.6 0.2 fusion.16
  299.8 10.8 %all-to-all-done = bf16[64,12,96]{2,1,0:T(8,128)(2,1)S(1)} async-done(((bf16[64,12,96]{2,1,0:T(8,128)(2,1)}), bf16[64,12,96]{2,1,0:T(8,128)(2,1)S(1)}, u32[]{:S(2)}, u32[]{:S(2)}) %all-to-all-start) | async-done | bytes 147488 | tf_op jit(solution)/shard_map/all_to_all | solution.py:56
  310.6 0.3 all_to_all.17
  310.9 0.4 fusion.39
  311.4 29.1 %all-reduce.1 = bf16[24,6144]{1,0:T(8,128)(2,1)S(1)} all-reduce(f32[24,6144]{1,0:T(8,128)S(1)} %fusion.39), channel_id=1, replica_groups=mesh['expert'=8,'tensor'=64] {'expert'}, use_global_device_ids=true, to_apply=%region_2.3 | all-reduce | flops 147456 | bytes 884736 | tf_op jit(solution)/shard_map/psum | solution.py:64
  340.4 0.6 dynamic-slice_convert_fusion
  (21 shorter events, 0.4 us)
Async XLA Ops:
  6.5 141.0 %copy-start = (bf16[1,6144,128]{2,1,0:T(8,128)(2,1)S(1)}, bf16[1,6144,128]{2,1,0:T(8,128)(2,1)}, u32[]{:S(2)}) copy-start(bf16[1,6144,128]{2,1,0:T(8,128)(2,1)} %param.9) | copy-start | bytes 4718596
  6.5 127.3 %all-gather.6.cloned.1.call-start = ((), (), s32[]{:S(2)}) async-start(), calls=%async_computation.2 | async-start | bytes 12779520 | tf_op jit(solution)/shard_map/all_gather | solution.py:47
  9.9 271.4 %all-gather.4.cloned.1.call-start = ((), (), s32[]{:S(2)}) async-start(), calls=%async_computation.1 | async-start | bytes 12779520 | tf_op jit(solution)/shard_map/all_gather | solution.py:51
  147.5 6.4 %copy-start.1 = (bf16[768,6144]{1,0:T(8,128)(2,1)S(1)}, bf16[768,6144]{1,0:T(8,128)(2,1)}, u32[]{:S(2)}) copy-start(bf16[768,6144]{1,0:T(8,128)(2,1)} %reshape.78) | copy-start | bytes 28311556
  147.6 6.9 %copy-start.4 = (bf16[1,6144,128]{2,1,0:T(8,128)(2,1)S(1)}, bf16[1,6144,128]{2,1,0:T(8,128)(2,1)}, u32[]{:S(2)}) copy-start(bf16[1,6144,128]{2,1,0:T(8,128)(2,1)} %param.10) | copy-start | bytes 4718596
  154.4 3.3 copy-start.3
  154.4 126.9 %copy-start.2 = (bf16[1,96,8192]{2,1,0:T(8,128)(2,1)S(1)}, bf16[1,96,8192]{2,1,0:T(8,128)(2,1)}, u32[]{:S(2)}) copy-start(bf16[1,96,8192]{2,1,0:T(8,128)(2,1)} %param.11) | copy-start | bytes 4718596
  290.8 19.7 %all-to-all-start = ((bf16[64,12,96]{2,1,0:T(8,128)(2,1)}), bf16[64,12,96]{2,1,0:T(8,128)(2,1)S(1)}, u32[]{:S(2)}, u32[]{:S(2)}) async-start(bf16[64,12,96]{2,1,0:T(8,128)(2,1)} %all_to_all.14), calls=%async_computation | async-start | bytes 524288 | tf_op jit(solution)/shard_map/all_to_all | solution.py:56
Sparse Core Ops, SparseCore 0:
  10.4 123.3 all-gather.5
  157.8 123.4 all-gather.3
where the time goes:
time: 350 us; the launch traced here: 348 us
  waiting for transfers between devices  258 us (74%)
  blocking collectives  29.1 us (8%)
  matrix products  20.7 us (6%)
  local copies, waits for them, and re-layouts  16.8 us (5%)
  between operations  13.5 us (4%)
  starting transfers between devices  8.6 us (2%)
    all_gather x1, waiting for transfers between devices, local(): shard_piece = lax.all_gather(picked, 'tensor', axis=0, tiled=True)  124 us
    all_gather x1, waiting for transfers between devices, local(): gathered = lax.all_gather(hidden, 'tensor', axis=1, tiled=True)  124 us
    psum x1, blocking collectives, local(): summed_all = lax.psum(contribution, 'expert')  29.1 us
    unnamed x11, local copies, waits for them, and re-layouts  14.5 us
    all_to_all x1, waiting for transfers between devices, local(): lax.all_to_all(outputs, 'tensor', split_axis=0, concat_axis=1, tiled=True)  10.8 us
    dot_general x1, matrix products, local(): lax.dot_general(gathered, w_down, (((1,), (1,)), ((), ())), preferred_ele...  8.57 us
    all_to_all x1, starting transfers between devices, local(): lax.all_to_all(outputs, 'tensor', split_axis=0, concat_axis=1, tiled=True)  8.56 us
  transfers between devices with their start and end apart: 3, of which 3 were waited for; matrix products, arithmetic and copies ran while one was open for 0% of the time, Pallas kernels for 0%

commit v1 on v0

v1 whole, which is shorter than its diff:
```python
import functools

import jax
import jax.numpy as jnp
from jax import lax
from jax.experimental import pallas as pl
from jax.experimental.pallas import tpu as pltpu
from jax.sharding import PartitionSpec as P

MESH = pl.DeviceIdType.MESH
R = 8
NX = 4
PIECE = 1536
WIDE = PIECE + 128
ROWS = 96
SLOTS = 768
HALF = 48
F32, BF16 = jnp.float32, jnp.bfloat16


def mod(a, n):
    return lax.rem(a + 4 * n, n)


def kernel(own_ref, wg_ref, wu_ref, wd_ref, wall_ref, out_ref,
           ph1, xin, xo, wgu, wab, hacc, hg, psend, precv, sumt, fsend, frecv,
           loc, r1, s1, r2, s2, rx, sx, rs, ss, wr, ws, hr, hs, pr, ps, fr, fs):
    e, t = lax.axis_index("expert"), lax.axis_index("tensor")
    y, z = t // R, lax.rem(t, R)
    x, c = e // 2, lax.rem(e, 2)
    d = 1 - 2 * c
    pos1, pos2 = (z, y), (y, z)
    sib = x * 2 + 1 - c
    xdev = (mod(x + 1, NX) * 2 + c, mod(x - 1, NX) * 2 + c)
    quarter = lax.rem(x, 2) * 2 + c

    def on_z(p):
        return (e, y * R + mod(p, R))

    def on_y(p):
        return (e, mod(p, R) * R + z)

    dev1, dev2 = (on_z, on_y), (on_y, on_z)

    def remote(src, dst, send, recv, dev):
        return pltpu.make_async_remote_copy(
            src_ref=src, dst_ref=dst, send_sem=send, recv_sem=recv,
            device_id=dev, device_id_type=MESH)

    def waiter(ref, sem):
        return pltpu.make_async_copy(ref, ref, sem)

    loads = [pltpu.make_async_copy(wg_ref, wgu.at[:, pl.ds(0, 128)], loc.at[0]),
             pltpu.make_async_copy(wu_ref, wgu.at[:, pl.ds(128, 128)], loc.at[1])]
    for k in (0, 1):
        loads.append(pltpu.make_async_copy(own_ref.at[k], ph1.at[k, pos1[k]], loc.at[2 + k]))
    for one in loads:
        one.start()

    barrier = pltpu.get_barrier_semaphore()

    @pl.loop(1, R)
    def _(k):
        pl.semaphore_signal(barrier, inc=1, device_id=on_z(z + k), device_id_type=MESH)
        pl.semaphore_signal(barrier, inc=1, device_id=on_y(y + k), device_id_type=MESH)

    for dev in (xdev[0], xdev[1], sib):
        pl.semaphore_signal(barrier, inc=1, device_id=(dev, t), device_id_type=MESH)
    pl.semaphore_wait(barrier, 2 * (R - 1) + 3)

    def travel(s):
        way = (2 * lax.rem(s, 2) - 1) * d
        return way, (s + 1) // 2

    for k in (0, 1):
        me = pos1[k]
        remote(own_ref.at[k], ph1.at[k, me], s1.at[k, 0], r1.at[k, 1], dev1[k](me + d)).start()
        remote(own_ref.at[k], ph1.at[k, me], s1.at[k, 1], r1.at[k, 2], dev1[k](me - d)).start()

    @pl.loop(1, R)
    def _(s):
        way, far = travel(s)
        for k in (0, 1):
            blk = ph1.at[k, mod(pos1[k] - way * far, R)]
            waiter(blk, r1.at[k, s]).wait()

            @pl.when(s <= 5)
            def _():
                remote(blk, blk, s1.at[k, s + 1], r1.at[k, s + 2], dev1[k](pos1[k] + way)).start()

    for one in loads:
        one.wait()

    row = lax.broadcasted_iota(jnp.int32, (ROWS, 128), 0)
    col = lax.broadcasted_iota(jnp.int32, (ROWS, 128), 1)
    take = jnp.where(col == (row // 12) * 16 + lax.rem(row, 12), 1.0, 0.0).astype(BF16)
    for k in (0, 1):
        xin[k, pos2[k]] = jnp.dot(take, ph1[k].reshape(128, WIDE), preferred_element_type=F32).astype(BF16)

    def share(k, g, s):
        src = xin.at[k, g, :, pl.ds(0, PIECE)]
        remote(src, xo.at[k, 1, g], sx.at[k, s], rx.at[k, s], (xdev[k], t)).start()
        remote(src, xo.at[k, 0, g], ss.at[k, 0, s], rs.at[k, 0, s], (sib, t)).start()

    for k in (0, 1):
        me = pos2[k]
        blk = xin.at[k, me]
        remote(blk, blk, s2.at[k, 0], r2.at[k, 1], dev2[k](me + d)).start()
        remote(blk, blk, s2.at[k, 1], r2.at[k, 2], dev2[k](me - d)).start()
        share(k, me, 0)

    def arrive(s):
        way, far = travel(s)
        for k in (0, 1):
            g = mod(pos2[k] - way * far, R)
            blk = xin.at[k, g]
            waiter(blk, r2.at[k, s]).wait()

            @pl.when(s <= 5)
            def _():
                remote(blk, blk, s2.at[k, s + 1], r2.at[k, s + 2], dev2[k](pos2[k] + way)).start()

            share(k, g, s)

    def weights(k):
        ty, tz = mod(y + k, R), mod(z + k, R)
        remote(wd_ref.at[pl.ds(0, HALF), pl.ds(pl.multiple_of(ty * 1024, 1024), 1024)],
               wab.at[0, y], ws.at[0], wr.at[0], on_y(ty)).start()
        for j in range(R):
            remote(wd_ref.at[pl.ds(HALF, HALF), pl.ds(pl.multiple_of(j * 1024 + tz * 128, 128), 128)],
                   wab.at[1, z, :, pl.ds(j * 128, 128)], ws.at[1], wr.at[1], on_z(tz)).start()

    pltpu.make_async_copy(wd_ref.at[pl.ds(0, HALF), pl.ds(pl.multiple_of(y * 1024, 1024), 1024)],
                          wab.at[0, y], wr.at[0]).start()
    for j in range(R):
        pltpu.make_async_copy(wd_ref.at[pl.ds(HALF, HALF), pl.ds(pl.multiple_of(j * 1024 + z * 128, 128), 128)],
                              wab.at[1, z, :, pl.ds(j * 128, 128)], wr.at[1]).start()

    hacc[...] = jnp.zeros_like(hacc)

    def relay(s):
        way, far = travel(s)
        for k in (0, 1):
            g = mod(pos2[k] - way * far, R)
            blk = xo.at[k, 1, g]
            waiter(blk, rx.at[k, s]).wait()
            remote(blk, xo.at[k, 2, g], ss.at[k, 1, s], rs.at[k, 1, s], (sib, t)).start()

    def multiply(s):
        way, far = travel(s)
        even = lax.rem(s, 2) == 0
        other = jnp.where((s == 0) | (s == 7), s, jnp.where(even, s - 1, s + 1))

        for k in (0, 1):
            g = mod(pos2[k] - way * far, R)
            for j in (0, 1):
                waiter(xo.at[k, 2 * j, g], rs.at[k, j, other]).wait()

            def part(rows, q):
                first = pl.multiple_of(q * PIECE, PIECE)
                return jnp.dot(rows, wgu[pl.ds(first, PIECE), :], preferred_element_type=F32)

            acc = part(xin[k, g, :, pl.ds(0, PIECE)], quarter)
            acc += part(xo[k, 0, g], quarter + 1 - 2 * c)
            acc += part(xo[k, 1, g], lax.rem(quarter + 2, 4))
            acc += part(xo[k, 2, g], lax.rem(quarter + 2, 4) + 1 - 2 * c)
            gate, up = acc[:, :128], acc[:, 128:]
            hidden = (gate / (1.0 + jnp.exp(-gate)) * up).astype(BF16)
            slot = xin[k, g, :, pl.ds(PIECE, 128)].astype(F32)[:, 0:1]
            line = lax.broadcasted_iota(jnp.int32, (ROWS, 1), 0) // 12
            block = g * R + line if k == 0 else line * R + g
            goal = jnp.where(slot >= 0, block.astype(F32) * 12.0 + slot, -1.0)
            place = lax.broadcasted_iota(jnp.int32, (ROWS, SLOTS), 1).astype(F32)
            chosen = jnp.where(place == goal, 1.0, 0.0).astype(BF16)
            hacc[...] += lax.dot_general(chosen, hidden, (((0,), (0,)), ((), ())), preferred_element_type=F32)

    arrive(jnp.int32(1))

    @pl.loop(0, R + 1)
    def _(s):
        @pl.when(s + 2 < R)
        def _():
            arrive(s + 2)

        @pl.when(s + 1 < R)
        def _():
            weights(s + 1)

        @pl.when(s < R)
        def _():
            relay(s)

        @pl.when(s > 0)
        def _():
            multiply(s - 1)

    H2 = SLOTS // 2
    hpos, hdev = (z, y), (on_z, on_y)

    def piece(k, p, h):
        return hg.at[k, pl.ds(h * H2, H2), pl.ds(pl.multiple_of(mod(p, R) * 128, 128), 128)]

    done = hacc[...].astype(BF16)
    for k in (0, 1):
        hg[k, :, pl.ds(pl.multiple_of(hpos[k] * 128, 128), 128)] = done
    for h in (0, 1):
        for k in (0, 1):
            blk = piece(k, hpos[k], h)
            remote(blk, blk, hs.at[k, h, 0], hr.at[k, h, 1], hdev[k](hpos[k] + d)).start()
            remote(blk, blk, hs.at[k, h, 1], hr.at[k, h, 2], hdev[k](hpos[k] - d)).start()

    @pl.loop(1, R)
    def _(s):
        way, far = travel(s)
        for h in (0, 1):
            for k in (0, 1):
                blk = piece(k, hpos[k] - way * far, h)
                waiter(blk, hr.at[k, h, s]).wait()

                @pl.when(s <= 5)
                def _():
                    remote(blk, blk, hs.at[k, h, s + 1], hr.at[k, h, s + 2], hdev[k](hpos[k] + way)).start()

    for k in (0, 1):
        waiter(wab.at[k], wr.at[k]).wait()

    ppos, pdev = (y, z), (on_y, on_z)
    for k in (0, 1):
        @pl.loop(0, 3)
        def _(n):
            cols = pl.ds(pl.multiple_of(n * 256, 256), 256)
            part = lax.dot_general(wab[k].reshape(R * HALF, 1024), hg[k, cols, :], (((1,), (1,)), ((), ())),
                                   preferred_element_type=F32)
            psend[k, :, :, cols] = part.astype(BF16).reshape(R, HALF, 256)

        @pl.loop(1, R)
        def _(j):
            to = mod(ppos[k] + j, R)
            remote(psend.at[k, to], precv.at[k, ppos[k]], ps.at[k], pr.at[k], pdev[k](to)).start()

    sumt[...] = jnp.zeros_like(sumt)
    for k in (0, 1):
        waiter(precv.at[k, pl.ds(0, R - 1)], pr.at[k]).wait()
        precv[k, ppos[k]] = psend[k, ppos[k]]
        total = precv[k, 0].astype(F32)
        for j in range(1, R):
            total += precv[k, j].astype(F32)
        sumt[pl.ds(k * HALF, HALF), :] = total.astype(BF16)

    @pl.loop(0, 4)
    def _(n):
        r = lax.broadcasted_iota(jnp.int32, (256, SLOTS), 0) + n * 256
        at = lax.rem(r, 16)
        goal = jnp.where(at < 12, (r // 16) * 12 + at, -1)
        order = jnp.where(lax.broadcasted_iota(jnp.int32, (256, SLOTS), 1) == goal, 1.0, 0.0).astype(BF16)
        got = lax.dot_general(order, sumt[...], (((1,), (1,)), ((), ())), preferred_element_type=F32)
        fsend[pl.ds(n * 16, 16)] = got.astype(BF16).reshape(16, 16, 128)

    mine = e == y
    landing = frecv.at[z * R + e]

    @pl.loop(0, R * R)
    def _(b):
        here = jnp.logical_and(b == t, mine)

        @pl.when(here)
        def _():
            pltpu.make_async_copy(fsend.at[b], landing, fr).start()

        @pl.when(jnp.logical_not(here))
        def _():
            remote(fsend.at[b], landing, fs, fr, (y, b)).start()

    waiter(frecv, fr).wait()
    for n in range(R):
        got = frecv[pl.ds(n * R, R)].reshape(128, 128).astype(F32)
        mixed = jnp.dot(wall_ref[...], got, precision=lax.Precision.HIGHEST, preferred_element_type=F32)
        out_ref[:, pl.ds(n * 128, 128)] = mixed.astype(BF16)

    @pl.loop(0, R - 1)
    def _(s):
        for k in (0, 1):
            waiter(ph1.at[k, 0], s1.at[k, s]).wait()
            waiter(xin.at[k, 0], s2.at[k, s]).wait()
            for h in (0, 1):
                waiter(piece(k, 0, h), hs.at[k, h, s]).wait()

    @pl.loop(0, R)
    def _(s):
        for k in (0, 1):
            waiter(xo.at[k, 0, 0], sx.at[k, s]).wait()
            for j in (0, 1):
                waiter(xo.at[k, 0, 0], ss.at[k, j, s]).wait()

    for k in (0, 1):
        waiter(wab.at[k, pl.ds(0, R - 1)], ws.at[k]).wait()
        waiter(psend.at[k, pl.ds(0, R - 1)], ps.at[k]).wait()

    @pl.when(mine)
    def _():
        waiter(fsend.at[pl.ds(0, R * R - 1)], fs).wait()

    @pl.when(jnp.logical_not(mine))
    def _():
        waiter(fsend, fs).wait()


def local(tokens, expert_ids, gate_units, gate_weight, up_weight, down_weight):
    e = lax.axis_index("expert")
    quarter = lax.rem(e // 2, 2) * 2 + lax.rem(e, 2)
    rows = tokens.shape[0]
    flat = expert_ids.reshape(-1)
    before = jnp.arange(2 * rows)[None, :] < jnp.arange(2 * rows)[:, None]
    rank = jnp.sum(jnp.where(before & (flat[None, :] == flat[:, None]), 1, 0), axis=1).reshape(rows, 2)
    slot = jnp.sum(jnp.where(expert_ids == e, rank + 1, 0), axis=1) - 1
    units = gate_units.astype(F32)
    shares = units / jnp.sum(units, axis=1, keepdims=True)
    lane = jnp.arange(128)[None, :]
    goal = expert_ids * 16 + rank
    wall = jnp.where(lane == goal[:, 0:1], shares[:, 0:1], 0.0) + jnp.where(lane == goal[:, 1:2], shares[:, 1:2], 0.0)
    mine = lax.dynamic_slice_in_dim(tokens, quarter * PIECE, PIECE, 1)
    tag = jnp.broadcast_to(slot[:, None].astype(BF16), (rows, 128))
    own = jnp.concatenate([mine, tag], axis=1).reshape(2, 12, WIDE)
    own = jnp.pad(own, ((0, 0), (0, 4), (0, 0)))

    dma = pltpu.SemaphoreType.DMA
    anywhere = pl.BlockSpec(memory_space=pl.ANY)
    vmem = pl.BlockSpec(memory_space=pltpu.VMEM)
    out = pl.pallas_call(
        kernel,
        out_shape=jax.ShapeDtypeStruct((rows, 1024), BF16),
        in_specs=[vmem, anywhere, anywhere, anywhere, vmem],
        out_specs=vmem,
        scratch_shapes=[
            pltpu.VMEM((2, R, 16, WIDE), BF16),
            pltpu.VMEM((2, R, ROWS, WIDE), BF16),
            pltpu.VMEM((2, 3, R, ROWS, PIECE), BF16),
            pltpu.VMEM((4 * PIECE, 256), BF16),
            pltpu.VMEM((2, R, HALF, 1024), BF16),
            pltpu.VMEM((SLOTS, 128), F32),
            pltpu.VMEM((2, SLOTS, 1024), BF16),
            pltpu.VMEM((2, R, HALF, SLOTS), BF16),
            pltpu.VMEM((2, R, HALF, SLOTS), BF16),
            pltpu.VMEM((128, SLOTS), BF16),
            pltpu.VMEM((R * R, 16, 128), BF16),
            pltpu.VMEM((R * R, 16, 128), BF16),
            dma((4,)),
            dma((2, R)), dma((2, R)),
            dma((2, R)), dma((2, R)),
            dma((2, R)), dma((2, R)),
            dma((2, 2, R)), dma((2, 2, R)),
            dma((2,)), dma((2,)),
            dma((2, 2, R)), dma((2, 2, R)),
            dma((2,)), dma((2,)),
            dma, dma,
        ],
        compiler_params=pltpu.CompilerParams(
            collective_id=0, has_side_effects=True, vmem_limit_bytes=60 * 1024 * 1024),
    )(own, gate_weight[0], up_weight[0], down_weight[0], wall)
    return out.reshape(rows, R, 128)[:, :, :HALF * 2].reshape(rows, R * HALF * 2)


def solution(mesh):
    return jax.shard_map(
        local,
        mesh=mesh,
        in_specs=(
            P("tensor", None),
            P("tensor", None),
            P("tensor", None),
            P("expert", None, "tensor"),
            P("expert", None, "tensor"),
            P("expert", "tensor", None),
        ),
        out_specs=P("tensor", "expert"),
        check_vma=False,
    )
```

time: 350 us -> 145 us (0.41)
  waiting for transfers between devices: 258 us -> 0 us
  Pallas kernels: 0 us -> 136 us
  blocking collectives: 29.1 us -> 0 us
  matrix products: 20.7 us -> 0 us
  between operations: 13.5 us -> 0.04 us
  local copies, waits for them, and re-layouts: 16.8 us -> 4.29 us
  starting transfers between devices: 8.6 us -> 0 us
    all_gather x2 -> x0, waiting for transfers between devices: 247 us -> none  [the longest x1 124 us: local(): shard_piece = lax.all_gather(picked, 'tensor', axis=0, tiled=True)]
    pallas_call x0 -> x1, Pallas kernels: none -> 136 us  [local(): pl.pallas_call(kernel, out_shape=jax.ShapeDtypeStruct((rows, 1024), BF16)...]
    psum x1 -> x0, blocking collectives: 29.1 us -> none  [local(): summed_all = lax.psum(contribution, 'expert')]
    dot_general x7 -> x0, matrix products: 20.7 us -> none  [the longest x1 8.57 us: local(): lax.dot_general(gathered, w_down, (((1,), (1,)), ((), ())), preferred_ele...]
    unnamed x11 -> x4, local copies, waits for them, and re-layouts: 14.5 us -> 2.53 us
    all_to_all x1 -> x0, waiting for transfers between devices: 10.8 us -> none  [local(): lax.all_to_all(outputs, 'tensor', split_axis=0, concat_axis=1, tiled=True)]
    all_to_all x1 -> x0, starting transfers between devices: 8.56 us -> none  [local(): lax.all_to_all(outputs, 'tensor', split_axis=0, concat_axis=1, tiled=True)]
  transfers between devices with their start and end apart: 3 -> 0, of which waited for: 3 -> 0; matrix products, arithmetic and copies ran while one was open for 0% -> 0% of each run, Pallas kernels for 0% -> 0%
where the time goes in v1:
time: 145 us; the launch traced here: 143 us
  Pallas kernels  136 us (94%)
  local copies, waits for them, and re-layouts  4.29 us (3%)
  other arithmetic  2.97 us (2%)
    pallas_call x1, Pallas kernels, local(): pl.pallas_call(kernel, out_shape=jax.ShapeDtypeStruct((rows, 1024), BF16)...  136 us

profile of v1, /device:TPU:56, one launch (start us, length us, event | category | flops | bytes accessed | tf_op | source)
XLA Modules:
  0.0 143.4 jit_solution(6017884573654551300)
XLA Ops:
  0.0 0.0 copy-start
  0.0 1.0 copy-done
  1.0 0.8 copy.22
  1.7 0.1 eq.53
  1.8 0.2 select_reduce_fusion
  2.0 0.1 reshape.20
  2.1 0.1 copy.23
  2.2 0.7 multiply_add_fusion
  2.9 0.1 broadcast_in_dim.47
  3.0 0.7 pad.4.own_ref
  3.7 0.7 convert_reduce_fusion
  4.4 0.7 convert_divide_fusion
  5.1 0.7 select_add_fusion.wall_ref
  5.8 136.1 %shard_map.64 = bf16[24,1024]{1,0:T(8,128)(2,1)} custom-call(bf16[2,16,1664]{2,1,0:T(8,128)(2,1)} %pad.4.own_ref, bf16[6144,128]{1,0:T(8,128)(2,1)} %bitcast.14, bf16[6144,128]{1,0:T(8,128)(2,1)} %bitcast.15, bf16[96,8192]{1,0:T(8,128)(2,1)} %bitcast.16, f32[24,128]{1,0:T(8,128)} %select_add_fusion.wall_ref), custom_call_target="tpu_custom_call" | custom-call | tf_op jit(solution)/shard_map/pallas_call | solution.py:329
  141.9 0.8 copy.25
  142.7 0.7 reshape.23
  (6 shorter events, 0.1 us)
Async XLA Ops:
  0.0 1.0 copy-start

commit v2 on v1

v2 whole, which is shorter than its diff:
```python
import jax
import jax.numpy as jnp
from jax import lax
from jax.experimental import pallas as pl
from jax.experimental.pallas import tpu as pltpu
from jax.sharding import PartitionSpec as P

MESH = pl.DeviceIdType.MESH
R = 8
NX = 4
D = 6144
PIECE = 1408
BOTH = 256
OWN = PIECE + BOTH
WIDE = OWN + 128
ROWS = 96
CUT = ROWS // 2
SLOTS = 768
HS = SLOTS // 2
HALF = 48
F32, BF16 = jnp.float32, jnp.bfloat16


def mod(a, n):
    return lax.rem(a + 4 * n, n)


def iota(shape, axis):
    return lax.broadcasted_iota(jnp.int32, shape, axis)


def ones(test):
    return jnp.where(test, 1.0, 0.0)


def across(a, b, **how):
    return lax.dot_general(a, b, (((1,), (1,)), ((), ())), preferred_element_type=F32, **how)


def kernel(tok_ref, ids_ref, unit_ref, wg_ref, wu_ref, wd_ref, out_ref,
           ph1, phx, xin, xs, xx, wgu, wab, hacc, hg, psend, precv, sumt, order, wall, fsend, frecv,
           loc, r1, s1, x1, y1, r2, s2, rx, sx, rs, ss, rq, sq, wr, ws, hr, hs, pr, ps, fr, fs):
    e, t = lax.axis_index("expert"), lax.axis_index("tensor")
    y, z = t // R, lax.rem(t, R)
    x, c = e // 2, lax.rem(e, 2)
    d = 1 - 2 * c
    pos1, pos2 = (z, y), (y, z)
    sib = x * 2 + 1 - c
    xdev = (mod(x + 1, NX) * 2 + c, mod(x - 1, NX) * 2 + c)
    quarter = lax.rem(x, 2) * 2 + c

    def on_z(p):
        return (e, y * R + mod(p, R))

    def on_y(p):
        return (e, mod(p, R) * R + z)

    dev1, dev2 = (on_z, on_y), (on_y, on_z)

    def remote(src, dst, send, recv, dev):
        return pltpu.make_async_remote_copy(
            src_ref=src, dst_ref=dst, send_sem=send, recv_sem=recv,
            device_id=dev, device_id_type=MESH)

    def waiter(ref, sem):
        return pltpu.make_async_copy(ref, ref, sem)

    barrier = pltpu.get_barrier_semaphore()
    for dev in (on_z(z + 1), on_z(z - 1), on_y(y + 1), on_y(y - 1), (xdev[0], t), (xdev[1], t), (sib, t)):
        pl.semaphore_signal(barrier, inc=1, device_id=dev, device_id_type=MESH)

    first = pl.multiple_of(quarter * PIECE, 128)
    second = pl.multiple_of(4 * PIECE + c * BOTH, 128)
    blocks = []
    for k in (0, 1):
        rows = pl.ds(8 * k, 16)
        blocks.append(pltpu.make_async_copy(
            tok_ref.at[rows, pl.ds(first, PIECE)], ph1.at[k, pos1[k], :, pl.ds(0, PIECE)], loc.at[2 + k]))
        blocks.append(pltpu.make_async_copy(
            tok_ref.at[rows, pl.ds(second, BOTH)], ph1.at[k, pos1[k], :, pl.ds(PIECE, BOTH)], loc.at[4 + k]))
    loads = [pltpu.make_async_copy(wg_ref, wgu.at[:, pl.ds(0, 128)], loc.at[0]),
             pltpu.make_async_copy(wu_ref, wgu.at[:, pl.ds(128, 128)], loc.at[1])]
    for one in blocks + loads:
        one.start()

    tokens = ids_ref.shape[1]
    ids, units = ids_ref[...], unit_ref[...].astype(F32)
    shares = units / (units[0:1, :] + units[1:2, :])
    home = iota((128, tokens), 0) // 16
    named = (ones(home == ids[0:1, :]), ones(home == ids[1:2, :]))
    names = (named[0] + named[1]).astype(BF16)
    here, there = iota((tokens, tokens), 0), iota((tokens, tokens), 1)
    rank = across(ones(there < here).astype(BF16), names)
    used = across(ones(there == here).astype(BF16), names)
    weight = across(ones(there == here), named[0] * shares[0:1, :] + named[1] * shares[1:2, :],
                    precision=lax.Precision.HIGHEST)
    lane = iota((tokens, 128), 1)
    wall[...] = jnp.where(rank == lax.rem(lane, 16).astype(F32), weight, 0.0)
    slot = jnp.sum(jnp.where(lane == e * 16, jnp.where(used > 0.5, rank, -1.0), 0.0), axis=1, keepdims=True)
    tag = jnp.broadcast_to(slot, (tokens, 128))
    for k in (0, 1):
        ph1[k, pos1[k], :, pl.ds(OWN, 128)] = tag[8 * k:8 * k + 16].astype(BF16)

    for one in blocks:
        one.wait()
    pl.semaphore_wait(barrier, 7)

    def travel(s):
        way = (2 * lax.rem(s, 2) - 1) * d
        return way, (s + 1) // 2

    def early(k, p, s):
        remote(ph1.at[k, p, :, pl.ds(0, PIECE)], phx.at[k, p], y1.at[k, s], x1.at[k, s], (xdev[k], t)).start()

    for k in (0, 1):
        me = pos1[k]
        blk = ph1.at[k, me]
        remote(blk, blk, s1.at[k, 0], r1.at[k, 1], dev1[k](me + d)).start()
        remote(blk, blk, s1.at[k, 1], r1.at[k, 2], dev1[k](me - d)).start()
        early(k, me, 0)

    r = iota((512, HS), 0)
    at = lax.rem(r, 16)
    order[...] = ones(iota((512, HS), 1) == jnp.where(at < 12, (r // 16) * 12 + at, -1)).astype(BF16)

    @pl.loop(1, R)
    def _(s):
        way, far = travel(s)
        for k in (0, 1):
            p = mod(pos1[k] - way * far, R)
            blk = ph1.at[k, p]
            waiter(blk, r1.at[k, s]).wait()

            @pl.when(s <= 5)
            def _():
                remote(blk, blk, s1.at[k, s + 1], r1.at[k, s + 2], dev1[k](pos1[k] + way)).start()

            early(k, p, s)

    row, col = iota((ROWS, 128), 0), iota((ROWS, 128), 1)
    take = [ones(col == (row // 12) * 16 + 4 * k + lax.rem(row, 12)).astype(BF16) for k in (0, 1)]

    def share(k, g, s, h):
        rows = pl.ds(h * CUT, CUT)
        if s is not None:
            remote(xin.at[k, g, rows, pl.ds(0, PIECE)], xx.at[k, 0, g, rows], sx.at[k, h, s], rx.at[k, h, s],
                   (xdev[k], t)).start()
        s = 0 if s is None else s
        remote(xin.at[k, g, rows, pl.ds(0, OWN)], xs.at[k, g, rows], ss.at[k, h, s], rs.at[k, h, s], (sib, t)).start()

    for k in (0, 1):
        me = pos2[k]
        for h in (0, 1):
            blk = xin.at[k, me, pl.ds(h * CUT, CUT)]
            if h == 0:
                xin[k, me] = jnp.dot(take[k], ph1[k].reshape(128, WIDE), preferred_element_type=F32).astype(BF16)
            remote(blk, blk, s2.at[k, h, 0], r2.at[k, h, 1], dev2[k](me + d)).start()
            remote(blk, blk, s2.at[k, h, 1], r2.at[k, h, 2], dev2[k](me - d)).start()
    for k in (0, 1):
        for h in (0, 1):
            share(k, pos2[k], None, h)

    for one in loads:
        one.wait()

    def arrive(s):
        way, far = travel(s)
        for h in (0, 1):
            for k in (0, 1):
                g = mod(pos2[k] - way * far, R)
                blk = xin.at[k, g, pl.ds(h * CUT, CUT)]
                waiter(blk, r2.at[k, h, s]).wait()

                @pl.when(s <= 5)
                def _():
                    remote(blk, blk, s2.at[k, h, s + 1], r2.at[k, h, s + 2], dev2[k](pos2[k] + way)).start()

                share(k, g, s, h)

    def weights(k):
        ty, tz = mod(y + k, R), mod(z + k, R)
        remote(wd_ref.at[pl.ds(0, HALF), pl.ds(pl.multiple_of(ty * 1024, 1024), 1024)],
               wab.at[0, y], ws.at[0], wr.at[0], on_y(ty)).start()
        for j in range(R):
            remote(wd_ref.at[pl.ds(HALF, HALF), pl.ds(pl.multiple_of(j * 1024 + tz * 128, 128), 128)],
                   wab.at[1, z, :, pl.ds(j * 128, 128)], ws.at[1], wr.at[1], on_z(tz)).start()

    pltpu.make_async_copy(wd_ref.at[pl.ds(0, HALF), pl.ds(pl.multiple_of(y * 1024, 1024), 1024)],
                          wab.at[0, y], wr.at[0]).start()
    for j in range(R):
        pltpu.make_async_copy(wd_ref.at[pl.ds(HALF, HALF), pl.ds(pl.multiple_of(j * 1024 + z * 128, 128), 128)],
                              wab.at[1, z, :, pl.ds(j * 128, 128)], wr.at[1]).start()

    hacc[...] = jnp.zeros_like(hacc)

    def onward(k, g, s, h):
        blk = xx.at[k, 0, g, pl.ds(h * CUT, CUT)]
        remote(blk, xx.at[k, 1, g, pl.ds(h * CUT, CUT)], sq.at[k, h, s], rq.at[k, h, s], (sib, t)).start()

    def relay(s):
        way, far = travel(s)
        for h in (0, 1):
            for k in (0, 1):
                g = mod(pos2[k] - way * far, R)
                waiter(xx.at[k, 0, g, pl.ds(h * CUT, CUT)], rx.at[k, h, s]).wait()
                onward(k, g, s, h)

    def multiply(s):
        way, far = travel(s)
        even = lax.rem(s, 2) == 0
        other = jnp.where((s == 0) | (s == 7), s, jnp.where(even, s - 1, s + 1))

        for k in (0, 1):
            g = mod(pos2[k] - way * far, R)
            for h in (0, 1):
                waiter(xs.at[k, g, pl.ds(h * CUT, CUT)], rs.at[k, h, other]).wait()
                waiter(xx.at[k, 1, g, pl.ds(h * CUT, CUT)], rq.at[k, h, other]).wait()

            def part(rows, q, size=PIECE):
                return jnp.dot(rows, wgu[pl.ds(pl.multiple_of(q, 128), size), :], preferred_element_type=F32)

            beside, over = quarter + 1 - 2 * c, lax.rem(quarter + 2, 4)
            acc = part(xin[k, g, :, pl.ds(0, PIECE)], quarter * PIECE)
            acc += part(xin[k, g, :, pl.ds(PIECE, BOTH)], second, BOTH)
            acc += part(xs[k, g, :, pl.ds(0, PIECE)], beside * PIECE)
            acc += part(xs[k, g, :, pl.ds(PIECE, BOTH)], 4 * PIECE + (1 - c) * BOTH, BOTH)
            acc += part(xx[k, 0, g], over * PIECE)
            acc += part(xx[k, 1, g], (over + 1 - 2 * c) * PIECE)
            gate, up = acc[:, :128], acc[:, 128:]
            hidden = (gate / (1.0 + jnp.exp(-gate)) * up).astype(BF16)
            place = xin[k, g, :, pl.ds(OWN, 128)].astype(F32)[:, 0:1]
            line = iota((ROWS, 1), 0) // 12
            block = g * R + line if k == 0 else line * R + g
            goal = jnp.where(place >= 0, block.astype(F32) * 12.0 + place, -1.0)
            chosen = ones(iota((ROWS, SLOTS), 1).astype(F32) == goal).astype(BF16)
            hacc[...] += lax.dot_general(chosen, hidden, (((0,), (0,)), ((), ())), preferred_element_type=F32)

    arrive(jnp.int32(1))

    for k in (0, 1):
        @pl.loop(0, R)
        def _(s):
            waiter(phx.at[k, 0], x1.at[k, s]).wait()

        xx[k, 0, pos2[k]] = jnp.dot(take[k], phx[k].reshape(128, PIECE), preferred_element_type=F32).astype(BF16)
        for h in (0, 1):
            onward(k, pos2[k], 0, h)

    @pl.loop(0, R + 1)
    def _(s):
        @pl.when(s + 2 < R)
        def _():
            arrive(s + 2)

        @pl.when(s + 1 < R)
        def _():
            weights(s + 1)

        @pl.when(jnp.logical_and(s > 0, s < R))
        def _():
            relay(s)

        @pl.when(s > 0)
        def _():
            multiply(s - 1)

    hpos, hdev = (z, y), (on_z, on_y)
    ppos, pdev = (y, z), (on_y, on_z)

    def piece(k, p, h):
        return hg.at[k, pl.ds(h * HS, HS), pl.ds(pl.multiple_of(mod(p, R) * 128, 128), 128)]

    done = hacc[...].astype(BF16)
    for k in (0, 1):
        hg[k, :, pl.ds(pl.multiple_of(hpos[k] * 128, 128), 128)] = done
    for h in (0, 1):
        for k in (0, 1):
            blk = piece(k, hpos[k], h)
            remote(blk, blk, hs.at[k, h, 0], hr.at[k, h, 1], hdev[k](hpos[k] + d)).start()
            remote(blk, blk, hs.at[k, h, 1], hr.at[k, h, 2], hdev[k](hpos[k] - d)).start()

    def pass_on(h, s):
        way, far = travel(s)
        for k in (0, 1):
            blk = piece(k, hpos[k] - way * far, h)
            waiter(blk, hr.at[k, h, s]).wait()

            @pl.when(s <= 5)
            def _():
                remote(blk, blk, hs.at[k, h, s + 1], hr.at[k, h, s + 2], hdev[k](hpos[k] + way)).start()

    def partial(h):
        for k in (0, 1):
            for n in range(3):
                part = across(wab[k].reshape(R * HALF, 1024), hg[k, pl.ds(h * HS + n * 128, 128), :])
                psend[k, h, :, :, pl.ds(n * 128, 128)] = part.astype(BF16).reshape(R, HALF, 128)

            @pl.loop(1, R)
            def _(j):
                to = mod(ppos[k] + j, R)
                remote(psend.at[k, h, to], precv.at[k, h, ppos[k]], ps.at[k, h], pr.at[k, h], pdev[k](to)).start()

    mine = e == y
    landing = frecv.at[z * R + e]

    def finish(h):
        for k in (0, 1):
            waiter(precv.at[k, h, pl.ds(0, R - 1)], pr.at[k, h]).wait()
            precv[k, h, ppos[k]] = psend[k, h, ppos[k]]
            total = precv[k, h, 0].astype(F32)
            for j in range(1, R):
                total += precv[k, h, j].astype(F32)
            sumt[h, pl.ds(k * HALF, HALF), :] = total.astype(BF16)
        fsend[pl.ds(h * 32, 32)] = across(order[...], sumt[h]).astype(BF16).reshape(32, 16, 128)

        @pl.loop(h * 32, h * 32 + 32)
        def _(b):
            stays = jnp.logical_and(b == t, mine)

            @pl.when(stays)
            def _():
                pltpu.make_async_copy(fsend.at[b], landing, fr).start()

            @pl.when(jnp.logical_not(stays))
            def _():
                remote(fsend.at[b], landing, fs, fr, (y, b)).start()

    sumt[...] = jnp.zeros_like(sumt)

    @pl.loop(1, R + 2)
    def _(s):
        @pl.when(s < R)
        def _():
            pass_on(0, s)

        @pl.when(s == R - 1)
        def _():
            pass_on(1, s - 2)
            for k in (0, 1):
                waiter(wab.at[k], wr.at[k]).wait()
            partial(0)

        @pl.when(jnp.logical_and(s > 2, s != R - 1))
        def _():
            pass_on(1, s - 2)

    partial(1)
    finish(0)
    finish(1)

    waiter(frecv, fr).wait()
    for n in range(R):
        got = frecv[pl.ds(n * R, R)].reshape(128, 128).astype(F32)
        mixed = jnp.dot(wall[...], got, precision=lax.Precision.HIGHEST, preferred_element_type=F32)
        out_ref[:, pl.ds(n * 128, 128)] = mixed.astype(BF16)

    @pl.loop(0, R - 1)
    def _(s):
        for k in (0, 1):
            waiter(ph1.at[k, 0], s1.at[k, s]).wait()
            for h in (0, 1):
                waiter(xin.at[k, 0, pl.ds(0, CUT)], s2.at[k, h, s]).wait()
                waiter(piece(k, 0, h), hs.at[k, h, s]).wait()

    @pl.loop(0, R)
    def _(s):
        for k in (0, 1):
            waiter(phx.at[k, 0], y1.at[k, s]).wait()
            for h in (0, 1):
                waiter(xs.at[k, 0, pl.ds(0, CUT)], ss.at[k, h, s]).wait()
                waiter(xx.at[k, 0, 0, pl.ds(0, CUT)], sq.at[k, h, s]).wait()

                @pl.when(s > 0)
                def _():
                    waiter(xx.at[k, 0, 0, pl.ds(0, CUT)], sx.at[k, h, s]).wait()

    for k in (0, 1):
        waiter(wab.at[k, pl.ds(0, R - 1)], ws.at[k]).wait()
        for h in (0, 1):
            waiter(psend.at[k, h, pl.ds(0, R - 1)], ps.at[k, h]).wait()

    @pl.when(mine)
    def _():
        waiter(fsend.at[pl.ds(0, R * R - 1)], fs).wait()

    @pl.when(jnp.logical_not(mine))
    def _():
        waiter(fsend, fs).wait()


def local(tokens, expert_ids, gate_units, gate_weight, up_weight, down_weight):
    rows = tokens.shape[0]
    dma = pltpu.SemaphoreType.DMA
    anywhere = pl.BlockSpec(memory_space=pl.ANY)
    vmem = pl.BlockSpec(memory_space=pltpu.VMEM)
    out = pl.pallas_call(
        kernel,
        out_shape=jax.ShapeDtypeStruct((rows, 1024), BF16),
        in_specs=[anywhere, vmem, vmem, anywhere, anywhere, anywhere],
        out_specs=vmem,
        scratch_shapes=[
            pltpu.VMEM((2, R, 16, WIDE), BF16),
            pltpu.VMEM((2, R, 16, PIECE), BF16),
            pltpu.VMEM((2, R, ROWS, WIDE), BF16),
            pltpu.VMEM((2, R, ROWS, OWN), BF16),
            pltpu.VMEM((2, 2, R, ROWS, PIECE), BF16),
            pltpu.VMEM((D, 256), BF16),
            pltpu.VMEM((2, R, HALF, 1024), BF16),
            pltpu.VMEM((SLOTS, 128), F32),
            pltpu.VMEM((2, SLOTS, 1024), BF16),
            pltpu.VMEM((2, 2, R, HALF, HS), BF16),
            pltpu.VMEM((2, 2, R, HALF, HS), BF16),
            pltpu.VMEM((2, 128, HS), BF16),
            pltpu.VMEM((512, HS), BF16),
            pltpu.VMEM((rows, 128), F32),
            pltpu.VMEM((R * R, 16, 128), BF16),
            pltpu.VMEM((R * R, 16, 128), BF16),
            dma((6,)),
            dma((2, R)), dma((2, R)),
            dma((2, R)), dma((2, R)),
            dma((2, 2, R)), dma((2, 2, R)),
            dma((2, 2, R)), dma((2, 2, R)),
            dma((2, 2, R)), dma((2, 2, R)),
            dma((2, 2, R)), dma((2, 2, R)),
            dma((2,)), dma((2,)),
            dma((2, 2, R)), dma((2, 2, R)),
            dma((2, 2)), dma((2, 2)),
            dma, dma,
        ],
        compiler_params=pltpu.CompilerParams(
            collective_id=0, has_side_effects=True, vmem_limit_bytes=60 * 1024 * 1024),
    )(tokens, expert_ids.T, gate_units.T, gate_weight[0], up_weight[0], down_weight[0])
    return out.reshape(rows, R, 128)[:, :, :HALF * 2].reshape(rows, R * HALF * 2)


def solution(mesh):
    return jax.shard_map(
        local,
        mesh=mesh,
        in_specs=(
            P("tensor", None),
            P("tensor", None),
            P("tensor", None),
            P("expert", None, "tensor"),
            P("expert", None, "tensor"),
            P("expert", "tensor", None),
        ),
        out_specs=P("tensor", "expert"),
        check_vma=False,
    )
```

time: 145 us -> 138 us (0.952)
  other arithmetic: 2.97 us -> 0 us
  local copies, waits for them, and re-layouts: 4.29 us -> 1.53 us
    unnamed x4 -> x1, local copies, waits for them, and re-layouts: 2.53 us -> 0.81 us
where the time goes in v2:
time: 138 us; the launch traced here: 137 us
  Pallas kernels  136 us (99%)
  local copies, waits for them, and re-layouts  1.53 us (1%)
    pallas_call x1, Pallas kernels, local(): pl.pallas_call(kernel, out_shape=jax.ShapeDtypeStruct((rows, 1024), BF16)...  136 us

profile of v2, /device:TPU:56, one launch (start us, length us, event | category | flops | bytes accessed | tf_op | source)
XLA Modules:
  0.0 137.5 jit_solution(3240200786237399070)
XLA Ops:
  0.0 135.9 %shard_map.64 = bf16[24,1024]{1,0:T(8,128)(2,1)} custom-call(bf16[24,6144]{1,0:T(8,128)(2,1)} %tok_ref.1, s32[2,24]{1,0:T(2,128)} %bitcast.13, s32[2,24]{1,0:T(2,128)} %bitcast.14, bf16[6144,128]{1,0:T(8,128)(2,1)} %bitcast.8, bf16[6144,128]{1,0:T(8,128)(2,1)} %bitcast.9, bf16[96,8192]{1,0:T(8,128)(2,1)} %bitcast.10), custom_call_target="tpu_custom_call" | custom-call | tf_op jit(solution)/shard_map/pallas_call | solution.py:396
  135.9 0.8 copy.7
  136.7 0.7 reshape.7

commit v3 on v2

v3 whole, which is shorter than its diff:
```python
import jax
import jax.numpy as jnp
from jax import lax
from jax.experimental import pallas as pl
from jax.experimental.pallas import tpu as pltpu
from jax.sharding import PartitionSpec as P

MESH = pl.DeviceIdType.MESH
R = 8
NX = 4
D = 6144
PIECE = 1408
BOTH = 256
OWN = PIECE + BOTH
WIDE = OWN + 128
ROWS = 96
CUT = ROWS // 2
SLOTS = 768
HS = SLOTS // 2
HALF = 48
F32, BF16 = jnp.float32, jnp.bfloat16


def mod(a, n):
    return lax.rem(a + 4 * n, n)


def iota(shape, axis):
    return lax.broadcasted_iota(jnp.int32, shape, axis)


def ones(test):
    return jnp.where(test, 1.0, 0.0)


def across(a, b, **how):
    return lax.dot_general(a, b, (((1,), (1,)), ((), ())), preferred_element_type=F32, **how)


def kernel(tok_ref, ids_ref, unit_ref, wg_ref, wu_ref, wd_ref, out_ref,
           ph1, phx, xin, xs, xx, acc, wgu, wab, hacc, hg, psend, precv, sumt, order, wall, fsend, frecv,
           loc, r1, s1, x1, y1, r2, s2, rx, sx, rs, ss, rq, sq, wr, ws, hr, hs, pr, ps, fr, fs):
    e, t = lax.axis_index("expert"), lax.axis_index("tensor")
    y, z = t // R, lax.rem(t, R)
    x, c = e // 2, lax.rem(e, 2)
    d = 1 - 2 * c
    pos1, pos2 = (z, y), (y, z)
    sib = x * 2 + 1 - c
    xdev = (mod(x + 1, NX) * 2 + c, mod(x - 1, NX) * 2 + c)
    quarter = lax.rem(x, 2) * 2 + c

    def on_z(p):
        return (e, y * R + mod(p, R))

    def on_y(p):
        return (e, mod(p, R) * R + z)

    dev1, dev2 = (on_z, on_y), (on_y, on_z)

    def remote(src, dst, send, recv, dev):
        return pltpu.make_async_remote_copy(
            src_ref=src, dst_ref=dst, send_sem=send, recv_sem=recv,
            device_id=dev, device_id_type=MESH)

    def waiter(ref, sem):
        return pltpu.make_async_copy(ref, ref, sem)

    barrier = pltpu.get_barrier_semaphore()
    near = [on(p + hop) for on, p in ((on_z, z), (on_y, y)) for hop in (1, -1, 2, -2)]
    for dev in near + [(xdev[0], t), (xdev[1], t), (sib, t)]:
        pl.semaphore_signal(barrier, inc=1, device_id=dev, device_id_type=MESH)

    first = pl.multiple_of(quarter * PIECE, 128)
    second = pl.multiple_of(4 * PIECE + c * BOTH, 128)
    blocks = []
    for k in (0, 1):
        rows = pl.ds(8 * k, 16)
        blocks.append(pltpu.make_async_copy(
            tok_ref.at[rows, pl.ds(first, PIECE)], ph1.at[k, pos1[k], :, pl.ds(0, PIECE)], loc.at[2 + k]))
        blocks.append(pltpu.make_async_copy(
            tok_ref.at[rows, pl.ds(second, BOTH)], ph1.at[k, pos1[k], :, pl.ds(PIECE, BOTH)], loc.at[4 + k]))
    loads = [pltpu.make_async_copy(wg_ref, wgu.at[:, pl.ds(0, 128)], loc.at[0]),
             pltpu.make_async_copy(wu_ref, wgu.at[:, pl.ds(128, 128)], loc.at[1])]
    for one in blocks + loads:
        one.start()

    tokens = ids_ref.shape[1]
    ids, units = ids_ref[...], unit_ref[...].astype(F32)
    shares = units / (units[0:1, :] + units[1:2, :])
    home = iota((128, tokens), 0) // 16
    named = (ones(home == ids[0:1, :]), ones(home == ids[1:2, :]))
    names = (named[0] + named[1]).astype(BF16)
    here, there = iota((tokens, tokens), 0), iota((tokens, tokens), 1)
    rank = across(ones(there < here).astype(BF16), names)
    used = across(ones(there == here).astype(BF16), names)
    weight = across(ones(there == here), named[0] * shares[0:1, :] + named[1] * shares[1:2, :],
                    precision=lax.Precision.HIGHEST)
    lane = iota((tokens, 128), 1)
    wall[...] = jnp.where(rank == lax.rem(lane, 16).astype(F32), weight, 0.0)
    slot = jnp.sum(jnp.where(lane == e * 16, jnp.where(used > 0.5, rank, -1.0), 0.0), axis=1, keepdims=True)
    tag = jnp.broadcast_to(slot, (tokens, 128))
    for k in (0, 1):
        ph1[k, pos1[k], :, pl.ds(OWN, 128)] = tag[8 * k:8 * k + 16].astype(BF16)

    for one in blocks:
        one.wait()
    pl.semaphore_wait(barrier, 11)

    def travel(s):
        way = jnp.where(s == R - 1, d, 2 * lax.rem(s, 2) - 1)
        return way, (s + 1) // 2

    def goes_on(s):
        return (s <= 4) | ((s == 5) & (c == 0)) | ((s == 6) & (c == 1))

    def later(s):
        return jnp.minimum(s + 2, R - 1)

    def early(k, p, s):
        remote(ph1.at[k, p, :, pl.ds(0, PIECE)], phx.at[k, p], y1.at[k, s], x1.at[k, s], (xdev[k], t)).start()

    def pass_block(k, p, s, to):
        blk = ph1.at[k, p]
        remote(blk, blk, s1.at[k, s - 1], r1.at[k, s], dev1[k](to)).start()

    for k in (0, 1):
        me = pos1[k]
        for s, hop in ((1, 1), (2, -1), (3, 2), (4, -2)):
            pass_block(k, me, s, me + hop)
        early(k, me, 0)

    r = iota((512, HS), 0)
    at = lax.rem(r, 16)
    order[...] = ones(iota((512, HS), 1) == jnp.where(at < 12, (r // 16) * 12 + at, -1)).astype(BF16)

    @pl.loop(1, R)
    def _(s):
        way, far = travel(s)
        for k in (0, 1):
            me = pos1[k]
            p = mod(me - way * far, R)
            waiter(ph1.at[k, p], r1.at[k, s]).wait()

            @pl.when((s == 3) | (s == 4))
            def _():
                pass_block(k, p, s + 2, me + way)

            @pl.when(s == 3 + c)
            def _():
                pass_block(k, p, R - 1, me + 2 * way)

            early(k, p, s)

    row, col = iota((ROWS, 128), 0), iota((ROWS, 128), 1)
    take = [ones(col == (row // 12) * 16 + 4 * k + lax.rem(row, 12)).astype(BF16) for k in (0, 1)]

    def part_of(k, h):
        return pl.ds(k * ROWS + h * CUT, CUT)

    def share(k, s, h):
        rows = part_of(k, h)
        if not isinstance(s, int):
            remote(xin.at[s, rows, pl.ds(0, PIECE)], xx.at[0, s, rows], sx.at[k, h, s], rx.at[k, h, s],
                   (xdev[k], t)).start()
        remote(xin.at[s, rows, pl.ds(0, OWN)], xs.at[s, rows], ss.at[k, h, s], rs.at[k, h, s], (sib, t)).start()

    for k in (0, 1):
        me = pos2[k]
        xin[0, pl.ds(k * ROWS, ROWS)] = jnp.dot(
            take[k], ph1[k].reshape(128, WIDE), preferred_element_type=F32).astype(BF16)
        for h in (0, 1):
            rows = part_of(k, h)
            for s, hop in ((1, 1), (2, -1)):
                remote(xin.at[0, rows], xin.at[s, rows], s2.at[k, h, s - 1], r2.at[k, h, s], dev2[k](me + hop)).start()
    for k in (0, 1):
        for h in (0, 1):
            share(k, 0, h)

    for one in loads:
        one.wait()

    def arrive(s):
        way, far = travel(s)
        for h in (0, 1):
            for k in (0, 1):
                rows = part_of(k, h)
                waiter(xin.at[s, rows], r2.at[k, h, s]).wait()

                @pl.when(goes_on(s))
                def _():
                    remote(xin.at[s, rows], xin.at[later(s), rows], s2.at[k, h, later(s) - 1], r2.at[k, h, later(s)],
                           dev2[k](pos2[k] + way)).start()

                share(k, s, h)

    def weights(k):
        ty, tz = mod(y + k, R), mod(z + k, R)
        remote(wd_ref.at[pl.ds(0, HALF), pl.ds(pl.multiple_of(ty * 1024, 1024), 1024)],
               wab.at[0, y], ws.at[0], wr.at[0], on_y(ty)).start()
        for j in range(R):
            remote(wd_ref.at[pl.ds(HALF, HALF), pl.ds(pl.multiple_of(j * 1024 + tz * 128, 128), 128)],
                   wab.at[1, z, :, pl.ds(j * 128, 128)], ws.at[1], wr.at[1], on_z(tz)).start()

    pltpu.make_async_copy(wd_ref.at[pl.ds(0, HALF), pl.ds(pl.multiple_of(y * 1024, 1024), 1024)],
                          wab.at[0, y], wr.at[0]).start()
    for j in range(R):
        pltpu.make_async_copy(wd_ref.at[pl.ds(HALF, HALF), pl.ds(pl.multiple_of(j * 1024 + z * 128, 128), 128)],
                              wab.at[1, z, :, pl.ds(j * 128, 128)], wr.at[1]).start()

    hacc[...] = jnp.zeros_like(hacc)

    def onward(k, s, h):
        rows = part_of(k, h)
        remote(xx.at[0, s, rows], xx.at[1, s, rows], sq.at[k, h, s], rq.at[k, h, s], (sib, t)).start()

    def relay(s):
        for h in (0, 1):
            for k in (0, 1):
                waiter(xx.at[0, s, part_of(k, h)], rx.at[k, h, s]).wait()
                onward(k, s, h)

    def part(rows, q, size=PIECE):
        return jnp.dot(rows, wgu[pl.ds(pl.multiple_of(q, 128), size), :], preferred_element_type=F32)

    beside, over = quarter + 1 - 2 * c, lax.rem(quarter + 2, 4)

    def multiply_plane(s):
        for k in (0, 1):
            for h in (0, 1):
                waiter(xs.at[s, part_of(k, h)], rs.at[k, h, s]).wait()
        some = part(xin[s, :, pl.ds(0, PIECE)], quarter * PIECE)
        some += part(xin[s, :, pl.ds(PIECE, BOTH)], second, BOTH)
        some += part(xs[s, :, pl.ds(0, PIECE)], beside * PIECE)
        some += part(xs[s, :, pl.ds(PIECE, BOTH)], 4 * PIECE + (1 - c) * BOTH, BOTH)
        acc[s] = some

    def multiply(s):
        way, far = travel(s)
        for k in (0, 1):
            for h in (0, 1):
                waiter(xx.at[1, s, part_of(k, h)], rq.at[k, h, s]).wait()
        both = acc[s] + part(xx[0, s], over * PIECE)
        both += part(xx[1, s], (over + 1 - 2 * c) * PIECE)
        gate, up = both[:, :128], both[:, 128:]
        hidden = (gate / (1.0 + jnp.exp(-gate)) * up).astype(BF16)
        place = xin[s, :, pl.ds(OWN, 128)].astype(F32)[:, 0:1]
        at = iota((2 * ROWS, 1), 0)
        line = lax.rem(at, ROWS) // 12
        block = jnp.where(at < ROWS, mod(y - way * far, R) * R + line, line * R + mod(z - way * far, R))
        goal = jnp.where(place >= 0, block.astype(F32) * 12.0 + place, -1.0)
        chosen = ones(iota((2 * ROWS, SLOTS), 1).astype(F32) == goal).astype(BF16)
        hacc[...] += lax.dot_general(chosen, hidden, (((0,), (0,)), ((), ())), preferred_element_type=F32)

    arrive(jnp.int32(1))

    for k in (0, 1):
        @pl.loop(0, R)
        def _(s):
            waiter(phx.at[k, 0], x1.at[k, s]).wait()

        xx[0, 0, pl.ds(k * ROWS, ROWS)] = jnp.dot(
            take[k], phx[k].reshape(128, PIECE), preferred_element_type=F32).astype(BF16)
        for h in (0, 1):
            onward(k, 0, h)

    @pl.loop(0, R + 1)
    def _(s):
        @pl.when(s + 2 < R)
        def _():
            arrive(s + 2)

        @pl.when(s + 1 < R)
        def _():
            weights(s + 1)

        @pl.when(s < R)
        def _():
            multiply_plane(s)

        @pl.when(s > 0)
        def _():
            multiply(s - 1)

        @pl.when(jnp.logical_and(s > 0, s < R))
        def _():
            relay(s)

    hpos, hdev = (z, y), (on_z, on_y)
    ppos, pdev = (y, z), (on_y, on_z)

    def piece(k, p, h):
        return hg.at[k, pl.ds(h * HS, HS), pl.ds(pl.multiple_of(mod(p, R) * 128, 128), 128)]

    done = hacc[...].astype(BF16)
    for k in (0, 1):
        hg[k, :, pl.ds(pl.multiple_of(hpos[k] * 128, 128), 128)] = done
    for h in (0, 1):
        for k in (0, 1):
            blk = piece(k, hpos[k], h)
            for s, hop in ((1, 1), (2, -1)):
                remote(blk, blk, hs.at[k, h, s - 1], hr.at[k, h, s], hdev[k](hpos[k] + hop)).start()

    def pass_on(h, s):
        way, far = travel(s)
        for k in (0, 1):
            blk = piece(k, hpos[k] - way * far, h)
            waiter(blk, hr.at[k, h, s]).wait()

            @pl.when(goes_on(s))
            def _():
                remote(blk, blk, hs.at[k, h, later(s) - 1], hr.at[k, h, later(s)], hdev[k](hpos[k] + way)).start()

    def send_sum(k, h, q, far):
        way = 1 - 2 * q
        remote(psend.at[k, h, mod(ppos[k] + way * far, R)], precv.at[k, h, q, far - 1],
               ps.at[k, h, q * 4 + far - 1], pr.at[k, h, q * 4 + far - 1], pdev[k](ppos[k] + way)).start()

    def partial(h):
        for k in (0, 1):
            some = across(wab[k].reshape(R * HALF, 1024), hg[k, pl.ds(h * HS, HS), :])
            psend[k, h] = some.astype(BF16).reshape(R, HALF, HS)
            for q in (0, 1):
                @pl.when(c == q)
                def _():
                    send_sum(k, h, q, 4)

                @pl.when(c != q)
                def _():
                    send_sum(k, h, q, 3)

    def add_on(h, far):
        for k in (0, 1):
            for q in (0, 1):
                @pl.when((far < 3) | (c == q))
                def _():
                    own = mod(ppos[k] + (1 - 2 * q) * far, R)
                    waiter(precv.at[k, h, q, far], pr.at[k, h, q * 4 + far]).wait()
                    psend[k, h, own] = (psend[k, h, own].astype(F32) + precv[k, h, q, far].astype(F32)).astype(BF16)
                    send_sum(k, h, q, far)

    mine = e == y
    landing = frecv.at[z * R + e]

    def finish(h):
        for k in (0, 1):
            total = psend[k, h, ppos[k]].astype(F32)
            for q in (0, 1):
                waiter(precv.at[k, h, q, 0], pr.at[k, h, q * 4]).wait()
                total += precv[k, h, q, 0].astype(F32)
            sumt[h, pl.ds(k * HALF, HALF), :] = total.astype(BF16)
        fsend[pl.ds(h * 32, 32)] = across(order[...], sumt[h]).astype(BF16).reshape(32, 16, 128)

        @pl.loop(0, 32)
        def _(i):
            b = h * 32 + lax.rem(y + 2 + i // R, 4) * R + lax.rem(z + 4 + i, R)
            stays = jnp.logical_and(b == t, mine)

            @pl.when(stays)
            def _():
                pltpu.make_async_copy(fsend.at[b], landing, fr).start()

            @pl.when(jnp.logical_not(stays))
            def _():
                remote(fsend.at[b], landing, fs, fr, (y, b)).start()

    sumt[...] = jnp.zeros_like(sumt)

    @pl.loop(0, 3)
    def _(i):
        for h in (0, 1):
            pass_on(h, 2 * i + 1)
            pass_on(h, 2 * i + 2)

    pass_on(0, jnp.int32(R - 1))
    for k in (0, 1):
        waiter(wab.at[k], wr.at[k]).wait()
    partial(0)
    pass_on(1, jnp.int32(R - 1))
    partial(1)
    for far in (3, 2, 1):
        for h in (0, 1):
            add_on(h, far)
    finish(0)
    finish(1)

    left, terms = wall[...], []
    for _ in range(3):
        terms.append(left.astype(BF16).astype(F32))
        left = left - terms[-1]
    terms = jnp.concatenate(terms, axis=0).astype(BF16)
    waiter(frecv, fr).wait()
    for n in range(R):
        mixed = jnp.dot(terms, frecv[pl.ds(n * R, R)].reshape(128, 128), preferred_element_type=F32)
        mixed = mixed[:tokens] + mixed[tokens:2 * tokens] + mixed[2 * tokens:]
        out_ref[:, pl.ds(n * 128, 128)] = mixed.astype(BF16)

    @pl.loop(0, R - 1)
    def _(s):
        for k in (0, 1):
            waiter(ph1.at[k, 0], s1.at[k, s]).wait()
            for h in (0, 1):
                waiter(xin.at[0, pl.ds(0, CUT)], s2.at[k, h, s]).wait()
                waiter(piece(k, 0, h), hs.at[k, h, s]).wait()

    @pl.loop(0, R)
    def _(s):
        for k in (0, 1):
            waiter(phx.at[k, 0], y1.at[k, s]).wait()
            for h in (0, 1):
                waiter(xs.at[0, pl.ds(0, CUT)], ss.at[k, h, s]).wait()
                waiter(xx.at[0, 0, pl.ds(0, CUT)], sq.at[k, h, s]).wait()

                @pl.when(s > 0)
                def _():
                    waiter(xx.at[0, 0, pl.ds(0, CUT)], sx.at[k, h, s]).wait()

    for k in (0, 1):
        waiter(wab.at[k, pl.ds(0, R - 1)], ws.at[k]).wait()
        for h in (0, 1):
            for q in (0, 1):
                for far in (0, 1, 2):
                    waiter(psend.at[k, h, 0], ps.at[k, h, q * 4 + far]).wait()

                @pl.when(c == q)
                def _():
                    waiter(psend.at[k, h, 0], ps.at[k, h, q * 4 + 3]).wait()

    @pl.when(mine)
    def _():
        waiter(fsend.at[pl.ds(0, R * R - 1)], fs).wait()

    @pl.when(jnp.logical_not(mine))
    def _():
        waiter(fsend, fs).wait()


def local(tokens, expert_ids, gate_units, gate_weight, up_weight, down_weight):
    rows = tokens.shape[0]
    dma = pltpu.SemaphoreType.DMA
    anywhere = pl.BlockSpec(memory_space=pl.ANY)
    vmem = pl.BlockSpec(memory_space=pltpu.VMEM)
    out = pl.pallas_call(
        kernel,
        out_shape=jax.ShapeDtypeStruct((rows, 1024), BF16),
        in_specs=[anywhere, vmem, vmem, anywhere, anywhere, anywhere],
        out_specs=vmem,
        scratch_shapes=[
            pltpu.VMEM((2, R, 16, WIDE), BF16),
            pltpu.VMEM((2, R, 16, PIECE), BF16),
            pltpu.VMEM((R, 2 * ROWS, WIDE), BF16),
            pltpu.VMEM((R, 2 * ROWS, OWN), BF16),
            pltpu.VMEM((2, R, 2 * ROWS, PIECE), BF16),
            pltpu.VMEM((R, 2 * ROWS, 256), F32),
            pltpu.VMEM((D, 256), BF16),
            pltpu.VMEM((2, R, HALF, 1024), BF16),
            pltpu.VMEM((SLOTS, 128), F32),
            pltpu.VMEM((2, SLOTS, 1024), BF16),
            pltpu.VMEM((2, 2, R, HALF, HS), BF16),
            pltpu.VMEM((2, 2, 2, 4, HALF, HS), BF16),
            pltpu.VMEM((2, 128, HS), BF16),
            pltpu.VMEM((512, HS), BF16),
            pltpu.VMEM((rows, 128), F32),
            pltpu.VMEM((R * R, 16, 128), BF16),
            pltpu.VMEM((R * R, 16, 128), BF16),
            dma((6,)),
            dma((2, R)), dma((2, R)),
            dma((2, R)), dma((2, R)),
            dma((2, 2, R)), dma((2, 2, R)),
            dma((2, 2, R)), dma((2, 2, R)),
            dma((2, 2, R)), dma((2, 2, R)),
            dma((2, 2, R)), dma((2, 2, R)),
            dma((2,)), dma((2,)),
            dma((2, 2, R)), dma((2, 2, R)),
            dma((2, 2, 8)), dma((2, 2, 8)),
            dma, dma,
        ],
        compiler_params=pltpu.CompilerParams(
            collective_id=0, has_side_effects=True, vmem_limit_bytes=60 * 1024 * 1024),
    )(tokens, expert_ids.T, gate_units.T, gate_weight[0], up_weight[0], down_weight[0])
    return out.reshape(rows, R, 128)[:, :, :HALF * 2].reshape(rows, R * HALF * 2)


def solution(mesh):
    return jax.shard_map(
        local,
        mesh=mesh,
        in_specs=(
            P("tensor", None),
            P("tensor", None),
            P("tensor", None),
            P("expert", None, "tensor"),
            P("expert", None, "tensor"),
            P("expert", "tensor", None),
        ),
        out_specs=P("tensor", "expert"),
        check_vma=False,
    )
```

time: 138 us -> 129 us (0.935)
  Pallas kernels: 136 us -> 127 us
    pallas_call x1, Pallas kernels: 136 us -> 127 us  [local(): pl.pallas_call(kernel, out_shape=jax.ShapeDtypeStruct((rows, 1024), BF16)...]
where the time goes in v3:
time: 129 us; the launch traced here: 128 us
  Pallas kernels  127 us (98%)
  local copies, waits for them, and re-layouts  1.53 us (1%)
    pallas_call x1, Pallas kernels, local(): pl.pallas_call(kernel, out_shape=jax.ShapeDtypeStruct((rows, 1024), BF16)...  127 us

profile of v3, /device:TPU:56, one launch (start us, length us, event | category | flops | bytes accessed | tf_op | source)
XLA Modules:
  0.0 128.3 jit_solution(14315303299400621141)
XLA Ops:
  0.0 126.8 %shard_map.64 = bf16[24,1024]{1,0:T(8,128)(2,1)} custom-call(bf16[24,6144]{1,0:T(8,128)(2,1)} %tok_ref.1, s32[2,24]{1,0:T(2,128)} %bitcast.13, s32[2,24]{1,0:T(2,128)} %bitcast.14, bf16[6144,128]{1,0:T(8,128)(2,1)} %bitcast.8, bf16[6144,128]{1,0:T(8,128)(2,1)} %bitcast.9, bf16[96,8192]{1,0:T(8,128)(2,1)} %bitcast.10), custom_call_target="tpu_custom_call" | custom-call | tf_op jit(solution)/shard_map/pallas_call | solution.py:442
  126.8 0.8 copy.7
  127.6 0.7 reshape.7

commit v4 on v3

--- a/solution.py
+++ b/solution.py
@@ -388,12 +388,6 @@
         terms.append(left.astype(BF16).astype(F32))
         left = left - terms[-1]
     terms = jnp.concatenate(terms, axis=0).astype(BF16)
-    waiter(frecv, fr).wait()
-    for n in range(R):
-        mixed = jnp.dot(terms, frecv[pl.ds(n * R, R)].reshape(128, 128), preferred_element_type=F32)
-        mixed = mixed[:tokens] + mixed[tokens:2 * tokens] + mixed[2 * tokens:]
-        out_ref[:, pl.ds(n * 128, 128)] = mixed.astype(BF16)
-
     @pl.loop(0, R - 1)
     def _(s):
         for k in (0, 1):
@@ -424,6 +418,14 @@
                 @pl.when(c == q)
                 def _():
                     waiter(psend.at[k, h, 0], ps.at[k, h, q * 4 + 3]).wait()
+
+    waiter(frecv, fr).wait()
+    parts = []
+    for n in range(R):
+        mixed = jnp.dot(terms, frecv[pl.ds(n * R, R)].reshape(128, 128), preferred_element_type=F32)
+        mixed = mixed[:tokens] + mixed[tokens:2 * tokens] + mixed[2 * tokens:]
+        parts.append(mixed[:, :2 * HALF])
+    out_ref[...] = jnp.concatenate(parts, axis=1).astype(BF16)
 
     @pl.when(mine)
     def _():
@@ -441,7 +443,7 @@
     vmem = pl.BlockSpec(memory_space=pltpu.VMEM)
     out = pl.pallas_call(
         kernel,
-        out_shape=jax.ShapeDtypeStruct((rows, 1024), BF16),
+        out_shape=jax.ShapeDtypeStruct((rows, R * HALF * 2), BF16),
         in_specs=[anywhere, vmem, vmem, anywhere, anywhere, anywhere],
         out_specs=vmem,
         scratch_shapes=[
@@ -477,7 +479,7 @@
         compiler_params=pltpu.CompilerParams(
             collective_id=0, has_side_effects=True, vmem_limit_bytes=60 * 1024 * 1024),
     )(tokens, expert_ids.T, gate_units.T, gate_weight[0], up_weight[0], down_weight[0])
-    return out.reshape(rows, R, 128)[:, :, :HALF * 2].reshape(rows, R * HALF * 2)
+    return out
 
 
 def solution(mesh):

time: 129 us -> 129 us (level)
  no operation moved by 1% of the time
where the time goes in v4:
time: 129 us; the launch traced here: 128 us
  Pallas kernels  126 us (98%)
  local copies, waits for them, and re-layouts  1.39 us (1%)
    pallas_call x1, Pallas kernels, local(): pl.pallas_call(kernel, out_shape=jax.ShapeDtypeStruct((rows, R * HALF * 2...  126 us

profile of v4, /device:TPU:56, one launch (start us, length us, event | category | flops | bytes accessed | tf_op | source)
XLA Modules:
  0.0 127.9 jit_solution(16322406109913260782)
XLA Ops:
  0.0 126.5 %shard_map.64 = bf16[24,768]{1,0:T(8,128)(2,1)} custom-call(bf16[24,6144]{1,0:T(8,128)(2,1)} %tok_ref.1, s32[2,24]{1,0:T(2,128)} %bitcast.8, s32[2,24]{1,0:T(2,128)} %bitcast.9, bf16[6144,128]{1,0:T(8,128)(2,1)} %bitcast.5, bf16[6144,128]{1,0:T(8,128)(2,1)} %bitcast.6, bf16[96,8192]{1,0:T(8,128)(2,1)} %bitcast.7), custom_call_target="tpu_custom_call" | custom-call | tf_op jit(solution)/shard_map/pallas_call | solution.py:444
  126.5 1.4 %copy.8 = bf16[24,768]{1,0:T(8,128)(2,1)} copy(bf16[24,768]{1,0:T(8,128)(2,1)} %shard_map.64) | data formatting | bytes 73728
